TPU v7x, 32 devices: a whole 2x2x4 slice. The times are simulated.
32 devices in a mesh: ctx: 4 (over y, core), ep: 8 (over z, x).
Axes of the slice: x: 2, y: 2, z: 4, core: 2. Of those that a mesh axis runs over, the one named last changes fastest.
Arguments:
- resid: bfloat16 [4096, 2048], P(('ctx', 'ep')), may hold values from -12 to 12
- mixed_qkv: bfloat16 [4096, 4096], P(('ctx', 'ep')), may hold values from -6 to 6
- out_gate: bfloat16 [4096, 2048], P(('ctx', 'ep')), may hold values from -6 to 6
- beta: float32 [16, 4096], P(None, ('ctx', 'ep')), may hold values from 0.001 to 0.95
- log_decay: float32 [16, 4096], P(None, ('ctx', 'ep')), may hold values from -1 to 0
- conv_weight: float32 [4, 4096], replicated, may hold values from -3 to 3
- head_gain: float32 [128], replicated, may hold values from 0.25 to 1.75
- moe_gain: float32 [2048], replicated, may hold values from 0.25 to 1.75
- routes: int32 [4096, 3], P(('ctx', 'ep')), may hold values from 0 to 7, all different within a row; in each aligned block of 128 rows (0 to 127, 128 to 255, ...) at most 60 rows name the same one
- route_gates: float32 [4096, 3], P(('ctx', 'ep')), may hold values from 0.1 to 1
- w_in: bfloat16 [8, 2048, 1024], P('ep', 'ctx'), may hold values from -0.125 to 0.125
- w_out: bfloat16 [8, 512, 2048], P('ep', None, 'ctx'), may hold values from -0.25 to 0.25
Outputs:
- mixer_out: bfloat16 [4096, 2048], P(('ctx', 'ep'))
- layer_out: bfloat16 [4096, 2048], P(('ctx', 'ep'))
Inputs may be any that keep to these rules, and one draw needn't show every extreme that they name: `routes`: in the rows of one device no expert is named more than 60 times, a bound that some block reaches.
All inputs are finite; a program needn't handle non-finite values.
Results may differ from a plain program's by a relative error of at most 0.0037.
Values may be sent and summed in bfloat16 or wider, within the bound.
No kernel may reach another device: no remote copies, remote signals or barrier semaphores. Data moves between devices by JAX's collectives and lax.ppermute only.
A program may use at most 320 MiB of HBM per device.

v0:
```python
import jax
import jax.numpy as jnp
from jax import lax
from jax.sharding import PartitionSpec as P

HK = 8
VALUE_HEAD_SET = 16
DK = 128
DV = 128
MOE_H = 512
CONV = 4
TOPK = 3
TOK_DEV = 128
precise = lax.Precision.HIGHEST


def from_behind(value, axis, steps):
    count = lax.axis_size(axis)
    leading, last = (max(0, -steps), min(count, count - steps))
    return lax.ppermute(value, axis, [(source, source + steps) for source in range(leading, last)])


def entering(value, axis, join, neutral, backward):
    count, mine = (lax.axis_size(axis), lax.axis_index(axis))
    pieces = jax.tree.map(lambda part: lax.all_gather(part, axis), value)
    if backward:
        pieces = jax.tree.map(lambda part: part[::-1], pieces)
        mine = count - 1 - mine
    so_far = jax.tree.map(
        lambda part, zero: jnp.full_like(part, 0) + jnp.asarray(zero, part.dtype), value, neutral
    )

    def lap(position, so_far):
        longer = join(so_far, jax.tree.map(lambda part: part[position], pieces))
        return jax.tree.map(lambda new, old: jnp.where(position < mine, new, old), longer, so_far)

    return lax.fori_loop(0, count - 1, lap, so_far)


def short_conv(padded, conv_weight, row_count):
    qkv_data = padded.astype(jnp.float32)
    conv_sum = jnp.zeros((row_count, qkv_data.shape[1]), jnp.float32)
    for offset in range(conv_weight.shape[0]):
        conv_sum = conv_sum + qkv_data[offset : offset + row_count] * conv_weight[offset]
    return jax.nn.silu(conv_sum)


def local_terms(conv_out, beta, log_decay):
    row_count = conv_out.shape[0]
    head_group = VALUE_HEAD_SET // HK
    queries = conv_out[:, : HK * DK].reshape(row_count, HK, DK)
    keys_hat = conv_out[:, HK * DK : 2 * HK * DK].reshape(row_count, HK, DK)
    values = conv_out[:, 2 * HK * DK :].reshape(row_count, VALUE_HEAD_SET, DV)
    queries = (
        queries
        * lax.rsqrt(jnp.sum(queries * queries, axis=-1, keepdims=True) + 1e-06)
        * DK ** (-0.5)
    )
    keys_hat = keys_hat * lax.rsqrt(jnp.sum(keys_hat * keys_hat, axis=-1, keepdims=True) + 1e-06)
    queries = jnp.repeat(queries, head_group, axis=1).transpose(1, 0, 2)
    keys_hat = jnp.repeat(keys_hat, head_group, axis=1).transpose(1, 0, 2)
    values = values.transpose(1, 0, 2)
    cumulative = jnp.cumsum(log_decay, axis=1)
    positions = jnp.arange(row_count)
    strict_mask = (positions[:, None] > positions[None, :])[None]
    causal_mask = (positions[:, None] >= positions[None, :])[None]
    log_gap = cumulative[:, :, None] - cumulative[:, None, :]
    fading = jnp.where(causal_mask, jnp.exp(jnp.where(causal_mask, log_gap, 0.0)), 0.0)
    key_key = jnp.einsum("htd,hsd->hts", keys_hat, keys_hat, precision=precise)
    mixing = jnp.where(strict_mask, beta[:, :, None] * fading * key_key, 0.0)
    identity_t = jnp.eye(row_count, dtype=jnp.float32)
    weights_solved = lax.linalg.triangular_solve(
        identity_t[None] + mixing, identity_t[None] * beta[:, :, None], left_side=True, lower=True
    )
    block_fade = jnp.exp(cumulative)
    tail_fade = jnp.exp(cumulative[:, -1:] - cumulative)
    fresh_vals = jnp.einsum("hts,hsv->htv", weights_solved, values, precision=precise)
    carried = jnp.einsum(
        "hts,hsk->htk", weights_solved, block_fade[:, :, None] * keys_hat, precision=precise
    )
    faded_keys = tail_fade[:, :, None] * keys_hat
    transition = block_fade[:, -1][:, None, None] * jnp.eye(DK, dtype=jnp.float32)[
        None
    ] - jnp.einsum("htj,htk->hjk", carried, faded_keys, precision=precise)
    state_add = jnp.einsum("htv,htk->hvk", fresh_vals, faded_keys, precision=precise)
    scores = fading * jnp.einsum("htd,hsd->hts", queries, keys_hat, precision=precise)
    return (queries, block_fade, scores, fresh_vals, carried, transition, state_add)


def head_outputs(queries, block_fade, scores, fresh_vals, carried, start_state):
    new_vals = fresh_vals - jnp.einsum("htk,hvk->htv", carried, start_state, precision=precise)
    from_state = jnp.einsum("htk,hvk->htv", queries, start_state, precision=precise)
    return block_fade[:, :, None] * from_state + jnp.einsum(
        "hts,hsv->htv", scores, new_vals, precision=precise
    )


def gated_norm(head_out, out_gate, head_gain):
    row_count = head_out.shape[1]
    per_token = head_out.transpose(1, 0, 2)
    scaled = (
        per_token
        * lax.rsqrt(jnp.mean(per_token * per_token, axis=-1, keepdims=True) + 1e-06)
        * head_gain
    )
    gate_vals = out_gate.astype(jnp.float32).reshape(row_count, VALUE_HEAD_SET, DV)
    return (
        (scaled * jax.nn.silu(gate_vals))
        .reshape(row_count, VALUE_HEAD_SET * DV)
        .astype(jnp.bfloat16)
    )


def compose(earlier, later):
    first_map, first_add = earlier
    second_map, second_add = later
    joined_map = jnp.einsum("hij,hjk->hik", first_map, second_map, precision=precise)
    joined_add = jnp.einsum("hvj,hjk->hvk", first_add, second_map, precision=precise) + second_add
    return (joined_map, joined_add)


def compose_back(higher, lower):
    return compose(lower, higher)


def expert_mlp(token_rows, weight_in, weight_out):
    projected = jnp.dot(token_rows, weight_in, preferred_element_type=jnp.float32)
    activated = (jax.nn.silu(projected[:, :MOE_H]) * projected[:, MOE_H:]).astype(jnp.bfloat16)
    return jnp.dot(activated, weight_out, preferred_element_type=jnp.float32).astype(jnp.bfloat16)


def shards(
    resid,
    mixed_qkv,
    out_gate,
    beta,
    log_decay,
    conv_weight,
    head_gain,
    moe_gain,
    routes,
    route_gates,
    w_in,
    w_out,
):
    row_count = mixed_qkv.shape[0]
    rim_rows = from_behind(mixed_qkv[row_count - CONV + 1 :], ("ctx", "ep"), 1)
    conv_out = short_conv(jnp.concatenate([rim_rows, mixed_qkv], axis=0), conv_weight, row_count)
    queries, block_fade, scores, fresh_vals, carried, transition, state_add = local_terms(
        conv_out, beta, log_decay
    )
    neutral = (
        jnp.broadcast_to(jnp.eye(DK, dtype=jnp.float32)[None], transition.shape),
        jnp.zeros_like(state_add),
    )
    within_group = entering((transition, state_add), "ep", compose, neutral, False)
    through_own = compose(within_group, (transition, state_add))
    after_own = entering((transition, state_add), "ep", compose_back, neutral, True)
    group_whole = compose(through_own, after_own)
    before_group = entering(group_whole, "ctx", compose, neutral, False)
    start_state = compose(before_group, within_group)[1]
    head_out = head_outputs(queries, block_fade, scores, fresh_vals, carried, start_state)
    mixer_out = gated_norm(head_out, out_gate, head_gain)
    residual_mid = resid.astype(jnp.float32) + mixer_out.astype(jnp.float32)
    moe_input = (
        residual_mid
        * lax.rsqrt(jnp.mean(residual_mid * residual_mid, axis=-1, keepdims=True) + 1e-06)
        * moe_gain
    ).astype(jnp.bfloat16)
    expert_count = lax.axis_size("ep")
    capacity = max(2, (5 * TOK_DEV * TOPK + 4 * expert_count - 1) // (4 * expert_count))
    slot_count = expert_count * capacity
    width = moe_input.shape[1]
    flat_routes = routes.reshape(-1)
    one_hot = (flat_routes[:, None] == jnp.arange(expert_count)[None, :]).astype(jnp.int32)
    earlier_same = jnp.cumsum(one_hot, axis=0) - one_hot
    slot_rank = jnp.sum(earlier_same * one_hot, axis=1)
    slot_ids = flat_routes * capacity + slot_rank
    selector = (slot_ids[None, :] == jnp.arange(slot_count)[:, None]).astype(jnp.int32)
    selector = jnp.sum(selector.reshape(slot_count, row_count, TOPK), axis=2).astype(jnp.bfloat16)
    send_rows = jnp.dot(selector, moe_input, preferred_element_type=jnp.float32).astype(
        jnp.bfloat16
    )
    send_rows = send_rows.reshape(expert_count, capacity, width)
    whole_in, whole_out = (
        lax.all_gather(w_in, "ctx", axis=1, tiled=True),
        lax.all_gather(w_out, "ctx", axis=2, tiled=True),
    )
    slot_rows = lax.all_to_all(send_rows, "ep", split_axis=0, concat_axis=0, tiled=True)
    flat_rows = slot_rows.reshape(-1, width)
    result_rows = expert_mlp(flat_rows, whole_in[0], whole_out[0]).reshape(slot_rows.shape)
    returned = lax.all_to_all(result_rows, "ep", split_axis=0, concat_axis=0, tiled=True)
    returned_flat = returned.reshape(slot_count, width)
    picked_rows = returned_flat[slot_ids].reshape(row_count, TOPK, width)
    combined = jnp.einsum("tk,tkd->td", route_gates, picked_rows.astype(jnp.float32))
    layer_out = (residual_mid + combined).astype(jnp.bfloat16)
    return (mixer_out, layer_out)


def solution(mesh):
    return jax.shard_map(
        shards,
        mesh=mesh,
        in_specs=(
            P(("ctx", "ep"), None),
            P(("ctx", "ep"), None),
            P(("ctx", "ep"), None),
            P(None, ("ctx", "ep")),
            P(None, ("ctx", "ep")),
            P(),
            P(),
            P(),
            P(("ctx", "ep"), None),
            P(("ctx", "ep"), None),
            P("ep", "ctx", None),
            P("ep", None, "ctx"),
        ),
        out_specs=(P(("ctx", "ep"), None), P(("ctx", "ep"), None)),
        check_vma=False,
    )
```

profile of v0, /device:TPU:0, one launch (start us, length us, event | category | flops | bytes accessed | tf_op | source)
XLA Modules:
  0.0 815.7 jit_solution(8747101318717336057)
XLA Ops:
  8.1 4.8 collective-permute-start
  18.2 4.6 divide_multiply_fusion
  28.0 158.6 %custom-call.3 = f32[16,1,128,128]{2,3,1,0:T(8,128)} custom-call(f32[16,1,128,128]{3,2,1,0:T(8,128)} %fusion.39), custom_call_target="InvertDiagBlocksLowerTriangular" | custom-call | tf_op jit(solution)/shard_map/triangular_solve | solution.py:72
  204.0 119.6 %all-gather.17.cloned.1.call-done = f32[128,128,128]{2,1,0:T(8,128)} async-done(((f32[16,128,128]{2,1,0:T(8,128)}), f32[128,128,128]{2,1,0:T(8,128)}) %all-gather.17.cloned.1.call-update) | async-done | bytes 8388624 | tf_op jit(solution)/shard_map/all_gather | solution.py:25
  323.6 7.7 rev.7
  331.4 117.5 %all-gather.15.cloned.1.call-done = f32[128,128,128]{2,1,0:T(8,128)} async-done(((f32[16,128,128]{2,1,0:T(8,128)}), f32[128,128,128]{2,1,0:T(8,128)}) %all-gather.15.cloned.1.call-update) | async-done | bytes 8388624 | tf_op jit(solution)/shard_map/all_gather | solution.py:25
  448.9 7.7 rev.6
  456.7 71.4 %while.46 = (s32[]{:T(128)}, f32[16,128,128]{1,2,0:T(8,128)S(1)}, f32[16,128,128]{1,2,0:T(8,128)}, s32[]{:T(128)}, f32[8,16,128,128]{3,2,1,0:T(8,128)}, /*index=5*/f32[8,16,128,128]{3,2,1,0:T(8,128)}, s32[]{:T(128)}, s32[]{:T(128)}) while((s32[]{:T(128)}, f32[16,128,128]{1,2,0:T(8,128)S(1)}, f32[16,128,128]{1,2,0:T(8,128)}, ...), condition=%wide.region_4.5_spmd.clone, body=%wide.region_3.4_spmd.clone.sunk | while | flops 806617088 | bytes 17828460 | solution.py:37
  459.6 4.1 fusion.118
  469.8 4.1 fusion.118
  480.0 4.1 fusion.118
  490.2 4.1 fusion.118
  500.4 4.1 fusion.118
  510.6 4.1 fusion.118
  520.8 4.1 fusion.118
  528.1 4.8 convolution_add_fusion.2
  533.0 37.2 %while.47 = (s32[]{:T(128)}, f32[16,128,128]{2,1,0:T(8,128)S(1)}, f32[16,128,128]{2,1,0:T(8,128)S(1)}, s32[]{:T(128)}, f32[8,16,128,128]{3,2,1,0:T(8,128)}, /*in...) while((s32[]{:T(128)}, f32[16,128,128]{2,1,0:T(8,128)S(1)}, f32[16,128,128]{2,1,0:T(8,128)S(1)}, ...), condition=%wide.region_6.7_spmd.clone, body=%wide.region_5.6_spmd.clone.sunk | while | flops 806354944 | bytes 10486890 | solution.py:37
  570.2 3.4 convolution_add_fusion.1
  592.2 14.2 %all-gather.21.cloned.1.call-done = f32[64,128,128]{2,1,0:T(8,128)} async-done(((f32[16,128,128]{2,1,0:T(8,128)}), f32[64,128,128]{2,1,0:T(8,128)}) %all-gather.21.cloned.1.call-update) | async-done | bytes 4194320 | tf_op jit(solution)/shard_map/all_gather | solution.py:25
  606.4 35.9 %all-gather.19.cloned.1.call-done = f32[64,128,128]{2,1,0:T(8,128)} async-done(((f32[16,128,128]{2,1,0:T(8,128)}), f32[64,128,128]{2,1,0:T(8,128)}) %all-gather.19.cloned.1.call-update) | async-done | bytes 4194320 | tf_op jit(solution)/shard_map/all_gather | solution.py:25
  642.3 21.5 %while.48 = (s32[]{:T(128)}, f32[16,128,128]{1,2,0:T(8,128)}, s32[]{:T(128)}, f32[4,16,128,128]{3,2,1,0:T(8,128)}, f32[4,16,128,128]{3,2,1,0:T(8,128)}, /*index=5*/s32[]{:T(128)}, s32[]{:T(128)}) while((s32[]{:T(128)}, f32[16,128,128]{1,2,0:T(8,128)}, s32[]{:T(128)}, f32[4,16,128,128]{3,2,1,0:T(8,128)}, ...), condition=%wide.region_8.9_spmd.clone, body=%wide.region_7.8_spmd.clone.sunk | while | flops 403701760 | bytes 11536483 | solution.py:37
  645.2 4.1 fusion.125
  652.3 4.2 fusion.125
  659.4 4.1 fusion.125
  663.9 3.5 convolution_add_fusion
  677.6 5.8 all-to-all-start
  684.0 48.1 %all-to-all-done = bf16[8,60,2048]{2,1,0:T(8,128)(2,1)S(1)} async-done(((bf16[8,60,2048]{2,1,0:T(8,128)(2,1)}), bf16[8,60,2048]{2,1,0:T(8,128)(2,1)S(1)}, u32[]{:S(2)}, u32[]{:S(2)}) %all-to-all-start) | async-done | bytes 1966112 | tf_op jit(solution)/shard_map/all_to_all | solution.py:189
  733.6 6.3 fusion.28
  739.9 3.4 convolution_convert_fusion.1
  744.9 4.7 all-to-all-start.1
  749.9 47.4 %all-to-all-done.1 = bf16[8,60,2048]{2,1,0:T(8,128)(2,1)} async-done(((bf16[8,60,2048]{2,1,0:T(8,128)(2,1)}), bf16[8,60,2048]{2,1,0:T(8,128)(2,1)}, u32[]{:S(2)}, u32[]{:S(2)}) %all-to-all-start.1) | async-done | bytes 1966112 | tf_op jit(solution)/shard_map/all_to_all | solution.py:192
  802.2 4.0 reshape.211
  (195 shorter events, 156.8 us)
Async XLA Ops:
  7.2 316.5 %all-gather.17.cloned.1.call-start = ((), (), s32[]{:S(2)}) async-start(), calls=%async_computation.5 | async-start | bytes 9437184 | tf_op jit(solution)/shard_map/all_gather | solution.py:25
  8.1 8.8 %collective-permute-start = (bf16[3,4096]{1,0:T(4,128)(2,1)S(1)}, bf16[3,4096]{1,0:T(4,128)(2,1)S(1)}, u32[]{:S(2)}, u32[]{:S(2)}) collective-permute-start(bf16[3,4096]{1,0:T(4,128)(2,1)S(1)} %slice.60), channel_id=1, source_target_pairs={{0,1},{1,2},{2,3},{3,4},{4,5},{5,6},{6,7},{7,8},{8,9},{9,10},{10,1... | collective-permute-start | bytes 73736 | tf_op jit(solution)/shard_map/ppermute | solution.py:20
  22.8 1.5 copy-start.2
  22.9 1.7 copy-start.17
  24.7 3.4 copy-start.11
  24.7 165.3 %slice-start = ((f32[128,4096]{0,1:T(8,128)}), f32[128,2048]{0,1:T(8,128)S(1)}, s32[]{:S(2)}) async-start(f32[128,4096]{0,1:T(8,128)} %copy-done.2), calls=%async_computation.8 | async-start | bytes 2097152 | tf_op jit(solution)/shard_map/slice | solution.py:53
  193.7 1.6 copy-start.5
  195.3 3.4 copy-start.13
  198.2 250.7 %all-gather.15.cloned.1.call-start = ((), (), s32[]{:S(2)}) async-start(), calls=%async_computation.4 | async-start | bytes 9437184 | tf_op jit(solution)/shard_map/all_gather | solution.py:25
  199.8 1.0 copy-start.7
  203.9 402.5 %all-gather.21.cloned.1.call-start = ((), (), s32[]{:S(2)}) async-start(), calls=%async_computation.7 | async-start | bytes 5242880 | tf_op jit(solution)/shard_map/all_gather | solution.py:25
  528.1 4.9 copy-start.1
  573.6 68.8 %all-gather.19.cloned.1.call-start = ((), (), s32[]{:S(2)}) async-start(), calls=%async_computation.6 | async-start | bytes 5242880 | tf_op jit(solution)/shard_map/all_gather | solution.py:25
  576.9 2.8 copy-start.19
  579.0 5.3 copy-start.16
  579.1 154.6 %all-gather.11.cloned.1.call-start = ((), (), s32[]{:S(2)}) async-start(), calls=%async_computation.2 | async-start | bytes 5242880 | tf_op jit(solution)/shard_map/all_gather | solution.py:186
  580.2 7.4 copy-start.12
  585.3 5.6 copy-start
  586.6 1.0 copy-start.3
  663.9 3.5 copy-start.4
  667.4 2.4 copy-start.6
  667.4 2.4 copy-start.8
  669.7 2.3 copy-start.15
  672.1 2.0 copy-start.14
  672.1 2.0 copy-start.21
  674.0 1.0 copy-start.10
  674.1 1.3 copy-start.18
  675.1 132.4 %copy-start.9 = (bf16[128,2048]{1,0:T(8,128)(2,1)}, bf16[128,2048]{1,0:T(8,128)(2,1)S(1)}, u32[]{:S(2)}) copy-start(bf16[128,2048]{1,0:T(8,128)(2,1)S(1)} %copy.117) | copy-start | bytes 1572868
  677.6 54.5 %all-to-all-start = ((bf16[8,60,2048]{2,1,0:T(8,128)(2,1)}), bf16[8,60,2048]{2,1,0:T(8,128)(2,1)S(1)}, u32[]{:S(2)}, u32[]{:S(2)}) async-start(bf16[8,60,2048]{2,1,0:T(8,128)(2,1)} %reshape.207), calls=%async_computation | async-start | bytes 4194304 | tf_op jit(solution)/shard_map/all_to_all | solution.py:189
  683.5 56.5 %all-gather.13.cloned.1.call-start = ((), (), s32[]{:S(2)}) async-start(), calls=%async_computation.3 | async-start | bytes 2621440 | tf_op jit(solution)/shard_map/all_gather | solution.py:187
  744.9 4.9 copy-start.20
  744.9 52.5 %all-to-all-start.1 = ((bf16[8,60,2048]{2,1,0:T(8,128)(2,1)}), bf16[8,60,2048]{2,1,0:T(8,128)(2,1)}, u32[]{:S(2)}, u32[]{:S(2)}) async-start(bf16[8,60,2048]{2,1,0:T(8,128)(2,1)} %reshape.209), calls=%async_computation.1 | async-start | bytes 4194304 | tf_op jit(solution)/shard_map/all_to_all | solution.py:192
Sparse Core Ops, SparseCore 0:
  198.3 125.2 all-gather.16
  325.8 123.1 all-gather.14
  573.7 32.6 all-gather.20
  607.8 34.4 all-gather.18
  643.7 34.4 all-gather.10
  685.5 23.0 all-gather.12
where the time goes:
time: 827 us; the launch traced here: 816 us
  waiting for transfers between devices  384 us (46%)
  other arithmetic  171 us (21%)
  matrix products  154 us (19%)
  local copies, waits for them, and re-layouts  75.2 us (9%)
  starting transfers between devices  15.9 us (2%)
  between operations  14.9 us (2%)
    all_gather x4, waiting for transfers between devices, entering(): pieces = jax.tree.map(lambda part: lax.all_gather(part, axis), value)  287 us
    another operation x1, other arithmetic, local_terms(): lax.linalg.triangular_solve(identity_t[None] + mixing, identity_t[None] *...  159 us
    dot_general x20, matrix products, compose(): jnp.einsum('hvj,hjk->hvk', first_add, second_map, precision=precise)  71.8 us
    all_to_all x1, waiting for transfers between devices, shards(): lax.all_to_all(send_rows, 'ep', split_axis=0, concat_axis=0, tiled=True)  48.1 us
    all_to_all x1, waiting for transfers between devices, shards(): lax.all_to_all(result_rows, 'ep', split_axis=0, concat_axis=0, tiled=True)  47.4 us
    dot_general x16, matrix products, compose(): jnp.einsum('hij,hjk->hik', first_map, second_map, precision=precise)  44.3 us
  transfers between devices with their start and end apart: 9, of which 6 were waited for; matrix products, arithmetic and copies ran while one was open for 9% of the time, Pallas kernels for 0%

commit v1 on v0

--- a/solution.py
+++ b/solution.py
@@ -2,6 +2,7 @@
 import jax.numpy as jnp
 from jax import lax
 from jax.sharding import PartitionSpec as P
+from jax.lax import axis_index, axis_size, ppermute
 
 HK = 8
 VALUE_HEAD_SET = 16
@@ -189,7 +190,21 @@
     slot_rows = lax.all_to_all(send_rows, "ep", split_axis=0, concat_axis=0, tiled=True)
     flat_rows = slot_rows.reshape(-1, width)
     result_rows = expert_mlp(flat_rows, whole_in[0], whole_out[0]).reshape(slot_rows.shape)
-    returned = lax.all_to_all(result_rows, "ep", split_axis=0, concat_axis=0, tiled=True)
+    t_next = axis_size("ep")
+    out_arr = axis_index("ep")
+    found_now, placed = (t_next, out_arr)
+    vec_out = result_rows.shape[0] // found_now
+    local_out = jnp.roll(result_rows, -placed * vec_out, axis=0)
+    carry = lax.slice_in_dim(local_out, 0, vec_out, axis=0)
+    xs_all = [carry]
+    for ii in range(1, found_now):
+        z_new = lax.slice_in_dim(local_out, ii * vec_out, (ii + 1) * vec_out, axis=0)
+        back = ppermute(
+            z_new, axis_name="ep", perm=[(c, (c + ii) % found_now) for c in range(found_now)]
+        )
+        xs_all.append(back)
+    next_value = jnp.concatenate(xs_all[::-1], axis=0)
+    returned = jnp.roll(next_value, (placed + 1) * xs_all[0].shape[0], axis=0)
     returned_flat = returned.reshape(slot_count, width)
     picked_rows = returned_flat[slot_ids].reshape(row_count, TOPK, width)
     combined = jnp.einsum("tk,tkd->td", route_gates, picked_rows.astype(jnp.float32))

time: 827 us -> 826 us (level)
  waiting for transfers between devices: 384 us -> 372 us
    all_to_all x1 -> x0, waiting for transfers between devices: 47.4 us -> none  [shards(): lax.all_to_all(result_rows, 'ep', split_axis=0, concat_axis=0, tiled=True)]
    ppermute x0 -> x7, waiting for transfers between devices: none -> 38 us  [shards(): ppermute(z_new, axis_name='ep', perm=[(c, (c + ii) % found_now) for c in...]
  transfers between devices with their start and end apart: 9 -> 15, of which waited for: 6 -> 10; matrix products, arithmetic and copies ran while one was open for 9% -> 10% of each run, Pallas kernels for 0% -> 0%
where the time goes in v1:
time: 826 us; the launch traced here: 817 us
  waiting for transfers between devices  372 us (45%)
  other arithmetic  175 us (21%)
  matrix products  153 us (19%)
  local copies, waits for them, and re-layouts  81.6 us (10%)
  starting transfers between devices  19 us (2%)
  between operations  15.1 us (2%)
    all_gather x4, waiting for transfers between devices, entering(): pieces = jax.tree.map(lambda part: lax.all_gather(part, axis), value)  285 us
    another operation x1, other arithmetic, local_terms(): lax.linalg.triangular_solve(identity_t[None] + mixing, identity_t[None] *...  158 us
    dot_general x20, matrix products, compose(): jnp.einsum('hvj,hjk->hvk', first_add, second_map, precision=precise)  71.8 us
    all_to_all x1, waiting for transfers between devices, shards(): lax.all_to_all(send_rows, 'ep', split_axis=0, concat_axis=0, tiled=True)  48.1 us
    dot_general x16, matrix products, compose(): jnp.einsum('hij,hjk->hik', first_map, second_map, precision=precise)  44.3 us
    ppermute x7, waiting for transfers between devices, shards(): ppermute(z_new, axis_name='ep', perm=[(c, (c + ii) % found_now) for c in...  38 us
  transfers between devices with their start and end apart: 15, of which 10 were waited for; matrix products, arithmetic and copies ran while one was open for 10% of the time, Pallas kernels for 0%

profile of v1, /device:TPU:0, one launch (start us, length us, event | category | flops | bytes accessed | tf_op | source)
XLA Modules:
  0.0 817.0 jit_solution(7295103470918051376)
XLA Ops:
  8.1 4.8 collective-permute-start
  18.4 4.6 divide_multiply_fusion
  29.7 158.0 %custom-call.3 = f32[16,1,128,128]{2,3,1,0:T(8,128)} custom-call(f32[16,1,128,128]{3,2,1,0:T(8,128)S(1)} %fusion.41), custom_call_target="InvertDiagBlocksLowerTriangular" | custom-call | tf_op jit(solution)/shard_map/triangular_solve | solution.py:73
  205.4 117.6 %all-gather.15.cloned.1.call-done = f32[128,128,128]{2,1,0:T(8,128)} async-done(((f32[16,128,128]{2,1,0:T(8,128)}), f32[128,128,128]{2,1,0:T(8,128)}) %all-gather.15.cloned.1.call-update) | async-done | bytes 8388624 | tf_op jit(solution)/shard_map/all_gather | solution.py:26
  323.0 7.7 rev.6
  330.7 117.5 %all-gather.17.cloned.1.call-done = f32[128,128,128]{2,1,0:T(8,128)} async-done(((f32[16,128,128]{2,1,0:T(8,128)}), f32[128,128,128]{2,1,0:T(8,128)}) %all-gather.17.cloned.1.call-update) | async-done | bytes 8388624 | tf_op jit(solution)/shard_map/all_gather | solution.py:26
  448.3 7.7 rev.7
  456.1 71.6 %while.46 = (s32[]{:T(128)}, f32[16,128,128]{1,2,0:T(8,128)S(1)}, f32[16,128,128]{1,2,0:T(8,128)}, s32[]{:T(128)}, f32[8,16,128,128]{3,2,1,0:T(8,128)}, /*index=5*/f32[8,16,128,128]{3,2,1,0:T(8,128)}, s32[]{:T(128)}, s32[]{:T(128)}) while((s32[]{:T(128)}, f32[16,128,128]{1,2,0:T(8,128)S(1)}, f32[16,128,128]{1,2,0:T(8,128)}, ...), condition=%wide.region_4.5_spmd.clone, body=%wide.region_3.4_spmd.clone.sunk | while | flops 806617088 | bytes 17828460 | solution.py:38
  459.2 4.1 fusion.121
  469.4 4.1 fusion.121
  479.6 4.1 fusion.121
  489.8 4.1 fusion.121
  499.9 4.1 fusion.121
  510.1 4.1 fusion.121
  520.3 4.1 fusion.121
  527.6 4.8 convolution_add_fusion.2
  532.5 37.2 %while.47 = (s32[]{:T(128)}, f32[16,128,128]{2,1,0:T(8,128)S(1)}, f32[16,128,128]{2,1,0:T(8,128)S(1)}, s32[]{:T(128)}, f32[8,16,128,128]{3,2,1,0:T(8,128)}, /*in...) while((s32[]{:T(128)}, f32[16,128,128]{2,1,0:T(8,128)S(1)}, f32[16,128,128]{2,1,0:T(8,128)S(1)}, ...), condition=%wide.region_6.7_spmd.clone, body=%wide.region_5.6_spmd.clone.sunk | while | flops 806354944 | bytes 10486890 | solution.py:38
  591.9 14.0 %all-gather.21.cloned.1.call-done = f32[64,128,128]{2,1,0:T(8,128)} async-done(((f32[16,128,128]{2,1,0:T(8,128)}), f32[64,128,128]{2,1,0:T(8,128)}) %all-gather.21.cloned.1.call-update) | async-done | bytes 4194320 | tf_op jit(solution)/shard_map/all_gather | solution.py:26
  605.9 36.0 %all-gather.19.cloned.1.call-done = f32[64,128,128]{2,1,0:T(8,128)} async-done(((f32[16,128,128]{2,1,0:T(8,128)}), f32[64,128,128]{2,1,0:T(8,128)}) %all-gather.19.cloned.1.call-update) | async-done | bytes 4194320 | tf_op jit(solution)/shard_map/all_gather | solution.py:26
  641.9 21.3 %while.48 = (s32[]{:T(128)}, f32[16,128,128]{1,2,0:T(8,128)}, s32[]{:T(128)}, f32[4,16,128,128]{3,2,1,0:T(8,128)}, f32[4,16,128,128]{3,2,1,0:T(8,128)}, /*index=5*/s32[]{:T(128)}, s32[]{:T(128)}) while((s32[]{:T(128)}, f32[16,128,128]{1,2,0:T(8,128)}, s32[]{:T(128)}, f32[4,16,128,128]{3,2,1,0:T(8,128)}, ...), condition=%wide.region_8.9_spmd.clone, body=%wide.region_7.8_spmd.clone.sunk | while | flops 403701760 | bytes 11536483 | solution.py:38
  644.8 4.1 fusion.128
  651.9 4.2 fusion.128
  659.0 4.1 fusion.128
  663.3 3.5 convolution_add_fusion
  677.1 5.8 all-to-all-start
  683.5 48.1 %all-to-all-done = bf16[8,60,2048]{2,1,0:T(8,128)(2,1)S(1)} async-done(((bf16[8,60,2048]{2,1,0:T(8,128)(2,1)}), bf16[8,60,2048]{2,1,0:T(8,128)(2,1)S(1)}, u32[]{:S(2)}, u32[]{:S(2)}) %all-to-all-start) | async-done | bytes 1966112 | tf_op jit(solution)/shard_map/all_to_all | solution.py:190
  733.3 6.3 fusion.28
  751.1 4.2 collective-permute-start.4
  759.0 4.9 collective-permute-done.2
  764.9 4.0 collective-permute-done.3
  768.9 26.0 %collective-permute-done.4 = bf16[1,60,2048]{2,1,0:T(8,128)(2,1)S(1)} collective-permute-done((bf16[1,60,2048]{2,1,0:T(8,128)(2,1)}, bf16[1,60,2048]{2,1,0:T(8,128)(2,1)S(1)}, u32[]{:S(2)}, u32[]{:S(2)}) %collective-permute-start.4) | collective-permute-done | bytes 245792 | tf_op jit(solution)/shard_map/ppermute | solution.py:202
  803.4 4.0 reshape.211
  (217 shorter events, 180.3 us)
Async XLA Ops:
  7.2 315.8 %all-gather.15.cloned.1.call-start = ((), (), s32[]{:S(2)}) async-start(), calls=%async_computation.3 | async-start | bytes 9437184 | tf_op jit(solution)/shard_map/all_gather | solution.py:26
  8.1 9.0 %collective-permute-start = (bf16[3,4096]{1,0:T(4,128)(2,1)S(1)}, bf16[3,4096]{1,0:T(4,128)(2,1)S(1)}, u32[]{:S(2)}, u32[]{:S(2)}) collective-permute-start(bf16[3,4096]{1,0:T(4,128)(2,1)S(1)} %slice.84), channel_id=1, source_target_pairs={{0,1},{1,2},{2,3},{3,4},{4,5},{5,6},{6,7},{7,8},{8,9},{9,10},{10,1... | collective-permute-start | bytes 73736 | tf_op jit(solution)/shard_map/ppermute | solution.py:21
  24.2 3.1 copy-start.17
  191.1 3.5 copy-start.6
  197.6 250.7 %all-gather.17.cloned.1.call-start = ((), (), s32[]{:S(2)}) async-start(), calls=%async_computation.4 | async-start | bytes 9437184 | tf_op jit(solution)/shard_map/all_gather | solution.py:26
  200.2 2.1 copy-start.7
  205.3 400.7 %all-gather.21.cloned.1.call-start = ((), (), s32[]{:S(2)}) async-start(), calls=%async_computation.6 | async-start | bytes 5242880 | tf_op jit(solution)/shard_map/all_gather | solution.py:26
  527.6 4.9 copy-start.1
  573.1 68.8 %all-gather.19.cloned.1.call-start = ((), (), s32[]{:S(2)}) async-start(), calls=%async_computation.5 | async-start | bytes 5242880 | tf_op jit(solution)/shard_map/all_gather | solution.py:26
  576.6 2.8 copy-start.19
  578.8 5.3 copy-start.16
  578.8 154.5 %all-gather.11.cloned.1.call-start = ((), (), s32[]{:S(2)}) async-start(), calls=%async_computation.1 | async-start | bytes 5242880 | tf_op jit(solution)/shard_map/all_gather | solution.py:187
  579.9 7.3 copy-start.13
  585.0 5.5 copy-start
  663.3 3.5 copy-start.3
  666.8 2.4 copy-start.5
  666.8 2.4 copy-start.9
  669.1 2.3 copy-start.15
  671.5 2.0 copy-start.14
  671.5 2.0 copy-start.21
  673.5 1.3 copy-start.18
  674.5 134.2 %copy-start.10 = (bf16[128,2048]{1,0:T(8,128)(2,1)}, bf16[128,2048]{1,0:T(8,128)(2,1)S(1)}, u32[]{:S(2)}) copy-start(bf16[128,2048]{1,0:T(8,128)(2,1)S(1)} %copy.117) | copy-start | bytes 1572868
  677.1 54.5 %all-to-all-start = ((bf16[8,60,2048]{2,1,0:T(8,128)(2,1)}), bf16[8,60,2048]{2,1,0:T(8,128)(2,1)S(1)}, u32[]{:S(2)}, u32[]{:S(2)}) async-start(bf16[8,60,2048]{2,1,0:T(8,128)(2,1)} %reshape.207), calls=%async_computation | async-start | bytes 4194304 | tf_op jit(solution)/shard_map/all_to_all | solution.py:190
  682.9 56.8 %all-gather.13.cloned.1.call-start = ((), (), s32[]{:S(2)}) async-start(), calls=%async_computation.2 | async-start | bytes 2621440 | tf_op jit(solution)/shard_map/all_gather | solution.py:188
  746.9 3.9 copy-start.20
  748.1 9.5 %collective-permute-start.1 = (bf16[1,60,2048]{2,1,0:T(8,128)(2,1)}, bf16[1,60,2048]{2,1,0:T(8,128)(2,1)}, u32[]{:S(2)}, u32[]{:S(2)}) collective-permute-start(bf16[1,60,2048]{2,1,0:T(8,128)(2,1)} %get-tuple-element.476), channel_id=1, source_target_pairs={{0,7},{1,0},{2,1},{3,2},{4,3},{5,4},{6,5},{7,6},{8,15},{9,8},{10,9... | collective-permute-start | bytes 737288 | tf_op jit(solution)/shard_map/ppermute | solution.py:202
  750.7 13.2 %collective-permute-start.2 = (bf16[1,60,2048]{2,1,0:T(8,128)(2,1)}, bf16[1,60,2048]{2,1,0:T(8,128)(2,1)}, u32[]{:S(2)}, u32[]{:S(2)}) collective-permute-start(bf16[1,60,2048]{2,1,0:T(8,128)(2,1)} %get-tuple-element.475), channel_id=1, source_target_pairs={{0,6},{1,7},{2,0},{3,1},{4,2},{5,3},{6,4},{7,5},{8,14},{9,15},{10,... | collective-permute-start | bytes 737288 | tf_op jit(solution)/shard_map/ppermute | solution.py:202
  751.0 17.9 %collective-permute-start.3 = (bf16[1,60,2048]{2,1,0:T(8,128)(2,1)}, bf16[1,60,2048]{2,1,0:T(8,128)(2,1)S(1)}, u32[]{:S(2)}, u32[]{:S(2)}) collective-permute-start(bf16[1,60,2048]{2,1,0:T(8,128)(2,1)} %get-tuple-element.474), channel_id=1, source_target_pairs={{0,5},{1,6},{2,7},{3,0},{4,1},{5,2},{6,3},{7,4},{8,13},{9,14},{10,... | collective-permute-start | bytes 737288 | tf_op jit(solution)/shard_map/ppermute | solution.py:202
  751.1 43.8 %collective-permute-start.4 = (bf16[1,60,2048]{2,1,0:T(8,128)(2,1)}, bf16[1,60,2048]{2,1,0:T(8,128)(2,1)S(1)}, u32[]{:S(2)}, u32[]{:S(2)}) collective-permute-start(bf16[1,60,2048]{2,1,0:T(8,128)(2,1)} %get-tuple-element.473), channel_id=1, source_target_pairs={{0,4},{1,5},{2,6},{3,7},{4,0},{5,1},{6,2},{7,3},{8,12},{9,13},{10,... | collective-permute-start | bytes 737288 | tf_op jit(solution)/shard_map/ppermute | solution.py:202
  755.3 41.0 %collective-permute-start.5 = (bf16[1,60,2048]{2,1,0:T(8,128)(2,1)}, bf16[1,60,2048]{2,1,0:T(8,128)(2,1)S(1)}, u32[]{:S(2)}, u32[]{:S(2)}) collective-permute-start(bf16[1,60,2048]{2,1,0:T(8,128)(2,1)} %get-tuple-element.472), channel_id=1, source_target_pairs={{0,3},{1,4},{2,5},{3,6},{4,7},{5,0},{6,1},{7,2},{8,11},{9,12},{10,... | collective-permute-start | bytes 737288 | tf_op jit(solution)/shard_map/ppermute | solution.py:202
  757.6 38.7 %collective-permute-start.6 = (bf16[1,60,2048]{2,1,0:T(8,128)(2,1)}, bf16[1,60,2048]{2,1,0:T(8,128)(2,1)S(1)}, u32[]{:S(2)}, u32[]{:S(2)}) collective-permute-start(bf16[1,60,2048]{2,1,0:T(8,128)(2,1)} %get-tuple-element.471), channel_id=1, source_target_pairs={{0,2},{1,3},{2,4},{3,5},{4,6},{5,7},{6,0},{7,1},{8,10},{9,11},{10,... | collective-permute-start | bytes 737288 | tf_op jit(solution)/shard_map/ppermute | solution.py:202
  763.9 32.5 %collective-permute-start.7 = (bf16[1,60,2048]{2,1,0:T(8,128)(2,1)S(1)}, bf16[1,60,2048]{2,1,0:T(8,128)(2,1)S(1)}, u32[]{:S(2)}, u32[]{:S(2)}) collective-permute-start(bf16[1,60,2048]{2,1,0:T(8,128)(2,1)S(1)} %get-tuple-element.470), channel_id=1, source_target_pairs={{0,1},{1,2},{2,3},{3,4},{4,5},{5,6},{6,7},{7,0},{8,9},{9,10},{10,1... | collective-permute-start | bytes 737288 | tf_op jit(solution)/shard_map/ppermute | solution.py:202
  (5 other events, 5.0 us)
Sparse Core Ops, SparseCore 0:
  197.7 125.2 all-gather.14
  325.1 123.1 all-gather.16
  573.2 32.6 all-gather.20
  607.4 34.5 all-gather.18
  643.3 34.4 all-gather.10
  684.9 23.0 all-gather.12
